TPU v7x, 32 devices: a whole 2x2x4 slice. The times are simulated.
32 devices in a mesh: group: 2 (over y), quad: 2 (over core), rows: 8 (over z, x).
Axes of the slice: x: 2, y: 2, z: 4, core: 2. Of those that a mesh axis runs over, the one named last changes fastest.
Arguments:
- solutions: bfloat16 [32, 20480, 128], P('quad', ('group', 'rows')), parts along dimension 1, may hold values from -24 to 24
- point_of_slot: int32 [64], P(('group', 'quad')), parts along dimension 0, may hold values from 0 to 31, each once
- mass_blocks: bfloat16 [160, 20, 128, 128], P(('group', 'rows')), parts along dimension 0, may hold values from -0.125 to 0.125
- block_cols: int32 [160, 20], P(('group', 'rows')), parts along dimension 0, may hold values from 0 to 79, as said below
- sources: bfloat16 [20480, 64], P(('group', 'rows')), parts along dimension 0, may hold values from -0.0625 to 0.0625
Outputs:
- mass_applied: bfloat16 [8, 20480, 128], P('quad', ('group', 'rows')), parts along dimension 1
- reduced: float32 [16, 64, 128], P(('group', 'quad')), parts along dimension 0
There are 2 independent parts, one for each index of `group`. A program takes and returns all parts, laid end to end along the dimension named above; each array names one. Nothing has to cross between parts.
Inputs may be any that keep to these rules, and one draw needn't show every extreme that they name: `point_of_slot`: each contour point sits in exactly one slot. `block_cols`: slot 0 of block row i holds i; every entry c of block row i has |c - i| <= 10; entries of a block row may repeat.
All inputs are finite; a program needn't handle non-finite values.
Results may differ from a plain program's by a relative error of at most 0.0063.
Values may be sent and summed in bfloat16 or wider, within the bound.
A program may use at most 128 MiB of HBM per device.

v0:
```python
import math

import jax
import jax.numpy as jnp
from jax import lax
from jax.sharding import PartitionSpec as P

MOMENTS = 8


def with_halo(block, sides, width):
    for axis, dim in sides:
        count = lax.axis_size(axis)
        forward = [(i, i + 1) for i in range(count - 1)]
        backward = [(target, source) for source, target in forward]
        low = lax.ppermute(
            lax.slice_in_dim(block, block.shape[dim] - width, None, axis=dim), axis, forward
        )
        high = lax.ppermute(lax.slice_in_dim(block, 0, width, axis=dim), axis, backward)
        block = jnp.concatenate([low, block, high], axis=dim)
    return block


def local(solutions, point_of_slot, mass_blocks, block_cols, sources):
    local_points = solutions.shape[0]
    rows_here = solutions.shape[1]
    width = solutions.shape[2] // 2
    block_size = mass_blocks.shape[2]
    span_blocks = rows_here // block_size
    total_points = local_points * lax.axis_size("quad")
    theta = 2.0 * math.pi * (point_of_slot.astype(jnp.float32) + 0.5) / total_points
    powers = jnp.arange(1, MOMENTS + 1, dtype=jnp.float32)
    angles = powers[:, None] * theta[None, :]
    cosine = (jnp.cos(angles) / total_points).astype(jnp.bfloat16)
    sine = (jnp.sin(angles) / total_points).astype(jnp.bfloat16)
    weighting = jnp.concatenate(
        [jnp.concatenate([cosine, -sine], axis=1), jnp.concatenate([sine, cosine], axis=1)], axis=0
    )
    stacked = jnp.concatenate([solutions[:, :, :width], solutions[:, :, width:]], axis=0).reshape(
        2 * local_points, rows_here * width
    )
    product = jnp.dot(weighting, stacked, preferred_element_type=jnp.float32).reshape(
        2, MOMENTS, rows_here, width
    )
    partial_value = jnp.concatenate([product[0], product[1]], axis=2)
    summed = lax.psum_scatter(
        partial_value.astype(jnp.bfloat16), "quad", scatter_dimension=0, tiled=True
    )
    widened = with_halo(summed, (("rows", 1),), rows_here)
    owned = widened.shape[0]
    panel_blocks = widened.reshape(owned, 3 * span_blocks, block_size, 2 * width)
    offset = (lax.axis_index("rows") - 1) * span_blocks
    local_cols = block_cols - offset

    def add_slot(slot_index, accum):
        columns_now = lax.dynamic_index_in_dim(local_cols, slot_index, 1, keepdims=False)
        tiles = lax.dynamic_index_in_dim(mass_blocks, slot_index, 1, keepdims=False)
        chosen = jnp.take(panel_blocks, columns_now, axis=1)
        return accum + jnp.einsum(
            "bij,mbjc->mbic", tiles, chosen, preferred_element_type=jnp.float32
        )

    start = jnp.zeros((owned, span_blocks, block_size, 2 * width), jnp.float32)
    accum = lax.fori_loop(0, mass_blocks.shape[1], add_slot, start)
    mass_applied = accum.astype(jnp.bfloat16).reshape(owned, rows_here, 2 * width)
    term = jnp.einsum("nl,mnc->mlc", sources, mass_applied, preferred_element_type=jnp.float32)
    reduced = lax.psum(term, "rows")
    return (mass_applied, reduced)


def solution(mesh):
    in_specs = (
        P("quad", ("group", "rows"), None),
        P(("group", "quad")),
        P(("group", "rows"), None, None, None),
        P(("group", "rows"), None),
        P(("group", "rows"), None),
    )
    out_specs = (P("quad", ("group", "rows"), None), P(("group", "quad"), None, None))
    return jax.shard_map(local, mesh=mesh, in_specs=in_specs, out_specs=out_specs, check_vma=False)
```

profile of v0, /device:TPU:0, one launch (start us, length us, event | category | flops | bytes accessed | tf_op | source)
XLA Modules:
  0.0 360.4 jit_solution(8767919289996625870)
XLA Ops:
  8.2 9.6 %fusion.22 = (bf16[16,1280,64]{2,1,0:T(8,128)(2,1)}, bf16[16,1280,64]{2,1,0:T(8,128)(2,1)}) fusion(bf16[16,1280,128]{2,1,0:T(8,128)(2,1)} %param.7), kind=kLoop, calls=%fused_computation.37 | loop fusion | bytes 10485760 | tf_op jit(solution)/shard_map/slice | solution.py:39
  17.8 10.4 %pad_maximum_fusion = bf16[32,1280,64]{2,1,0:T(8,128)(2,1)} fusion(bf16[16,1280,64]{2,1,0:T(8,128)(2,1)} %get-tuple-element.138, bf16[16,1280,64]{2,1,0:T(8,128)(2,1)} %get-tuple-element.137), kind=kLoop, calls=%fused_computation.14 | loop fusion | flops 2621440 | bytes 10485760 | tf_op jit(solution)/shard_map/concatenate | solution.py:39
  28.2 11.0 %reshape.29 = bf16[32,81920]{1,0:T(8,128)(2,1)} reshape(bf16[32,1280,64]{2,1,0:T(8,128)(2,1)} %pad_maximum_fusion) | data formatting | bytes 10485760 | tf_op jit(solution)/shard_map/reshape | solution.py:39
  39.2 3.4 convolution_convert_fusion
  45.5 3.1 squeeze.20
  48.6 3.0 reshape.45
  51.6 4.3 %squeeze.21 = bf16[8,1280,64]{2,1,0:T(8,128)(2,1)} reshape(bf16[655360]{0:T(1024)(128)(2,1)} %reshape.45) | data formatting | bytes 2621440 | tf_op jit(solution)/shard_map/squeeze | solution.py:45
  55.9 4.7 %pad_maximum_fusion.2 = bf16[8,1280,128]{2,1,0:T(8,128)(2,1)} fusion(bf16[8,1280,64]{2,1,0:T(8,128)(2,1)} %squeeze.21, bf16[8,1280,64]{2,1,0:T(8,128)(2,1)S(1)} %squeeze.20), kind=kLoop, calls=%fused_computation.16 | loop fusion | flops 5242880 | bytes 5242880 | tf_op jit(solution)/shard_map/concatenate | solution.py:45
  60.6 13.0 %reduce-scatter.2.cloned.1.call-done = bf16[4,1280,128]{2,1,0:T(8,128)(2,1)} async-done(((bf16[8,1280,128]{2,1,0:T(8,128)(2,1)}), bf16[4,1280,128]{2,1,0:T(8,128)(2,1)}) %reduce-scatter.2.cloned.1.call-update) | async-done | bytes 1310736 | tf_op jit(solution)/shard_map/reduce_scatter | solution.py:46
  73.6 3.8 %collective-permute-start = (bf16[4,1280,128]{2,1,0:T(8,128)(2,1)}, bf16[4,1280,128]{2,1,0:T(8,128)(2,1)S(1)}, u32[]{:S(2)}, u32[]{:S(2)}) collective-permute-start(bf16[4,1280,128]{2,1,0:T(8,128)(2,1)} %reduce-scatter.2.cloned.1.call-done), channel_id=1, source_target_pairs={{0,1},{1,2},{2,3},{3,4},{4,5},{5,6},{6,7},{8,9},{9,10},{10,11},{11... | collective-permute-start | bytes 3932168 | tf_op jit(solution)/shard_map/ppermute | solution.py:16
  78.8 55.3 %collective-permute-done = bf16[4,1280,128]{2,1,0:T(8,128)(2,1)S(1)} collective-permute-done((bf16[4,1280,128]{2,1,0:T(8,128)(2,1)}, bf16[4,1280,128]{2,1,0:T(8,128)(2,1)S(1)}, u32[]{:S(2)}, u32[]{:S(2)}) %collective-permute-start) | collective-permute-done | bytes 1310752 | tf_op jit(solution)/shard_map/ppermute | solution.py:16
  134.1 3.1 pad_maximum_fusion.1
  137.2 139.2 %while.14 = (s32[]{:T(128)}, f32[4,10,128,128]{2,3,0,1:T(8,128)}, s32[10,20]{0,1:T(8,128)S(1)}, bf16[4,30,128,128]{3,2,1,0:T(8,128)(2,1)}, bf16[10,20,128,128]{3,2,1,0:T(8,128)(2,1)}, /*index=5*/s32[]{:T(128)}, s32[]{:T(128)}) while((s32[]{:T(128)}, f32[4,10,128,128]{2,3,0,1:T(8,128)}, s32[10,20]{0,1:T(8,128)S(1)}, ...), condition=%wide.region_2.3_spmd.clone, body=%wide.region_1.2_spmd.clone.sunk | while | flops 169739328 | bytes 9507599 | solution.py:64
  137.2 2.9 gather_fusion
  140.2 3.2 bitcast_add_fusion.2
  143.4 2.9 gather_fusion
  146.3 4.1 %bitcast_add_fusion.2 = f32[4,10,128,128]{2,3,0,1:T(8,128)} fusion(f32[4,10,128,128]{2,3,0,1:T(8,128)} %get-tuple-element.186, bf16[10,4,128,128]{3,2,1,0:T(8,128)(2,1)S(1)} %gather_fusion, pred[10]{0:T(512)(128)(4,1)S(1)} %get-tuple-element.177, pred[]{:T(512)S(6)} %compare.3, bf16[10,20,128,128]{3,2,1,0:T(8,128)(2,1)} %get-tuple-element.196, ...), kind=kOutput, calls=%fused_computation.1.clone.1 | convolution fusion | flops 169738240 | bytes 6881803 | tf_op jit(solution)/shard_map/while/body/eval_jaxpr/bij,mbjc->mbic/dot_general | solution.py:59
  150.4 2.9 gather_fusion
  153.3 4.1 %bitcast_add_fusion.2 = f32[4,10,128,128]{2,3,0,1:T(8,128)} fusion(f32[4,10,128,128]{2,3,0,1:T(8,128)} %get-tuple-element.186, bf16[10,4,128,128]{3,2,1,0:T(8,128)(2,1)S(1)} %gather_fusion, pred[10]{0:T(512)(128)(4,1)S(1)} %get-tuple-element.177, pred[]{:T(512)S(6)} %compare.3, bf16[10,20,128,128]{3,2,1,0:T(8,128)(2,1)} %get-tuple-element.196, ...), kind=kOutput, calls=%fused_computation.1.clone.1 | convolution fusion | flops 169738240 | bytes 6881803 | tf_op jit(solution)/shard_map/while/body/eval_jaxpr/bij,mbjc->mbic/dot_general | solution.py:59
  157.4 2.9 gather_fusion
  160.3 4.1 %bitcast_add_fusion.2 = f32[4,10,128,128]{2,3,0,1:T(8,128)} fusion(f32[4,10,128,128]{2,3,0,1:T(8,128)} %get-tuple-element.186, bf16[10,4,128,128]{3,2,1,0:T(8,128)(2,1)S(1)} %gather_fusion, pred[10]{0:T(512)(128)(4,1)S(1)} %get-tuple-element.177, pred[]{:T(512)S(6)} %compare.3, bf16[10,20,128,128]{3,2,1,0:T(8,128)(2,1)} %get-tuple-element.196, ...), kind=kOutput, calls=%fused_computation.1.clone.1 | convolution fusion | flops 169738240 | bytes 6881803 | tf_op jit(solution)/shard_map/while/body/eval_jaxpr/bij,mbjc->mbic/dot_general | solution.py:59
  164.4 2.9 gather_fusion
  167.3 4.1 %bitcast_add_fusion.2 = f32[4,10,128,128]{2,3,0,1:T(8,128)} fusion(f32[4,10,128,128]{2,3,0,1:T(8,128)} %get-tuple-element.186, bf16[10,4,128,128]{3,2,1,0:T(8,128)(2,1)S(1)} %gather_fusion, pred[10]{0:T(512)(128)(4,1)S(1)} %get-tuple-element.177, pred[]{:T(512)S(6)} %compare.3, bf16[10,20,128,128]{3,2,1,0:T(8,128)(2,1)} %get-tuple-element.196, ...), kind=kOutput, calls=%fused_computation.1.clone.1 | convolution fusion | flops 169738240 | bytes 6881803 | tf_op jit(solution)/shard_map/while/body/eval_jaxpr/bij,mbjc->mbic/dot_general | solution.py:59
  171.4 2.9 gather_fusion
  174.3 4.1 %bitcast_add_fusion.2 = f32[4,10,128,128]{2,3,0,1:T(8,128)} fusion(f32[4,10,128,128]{2,3,0,1:T(8,128)} %get-tuple-element.186, bf16[10,4,128,128]{3,2,1,0:T(8,128)(2,1)S(1)} %gather_fusion, pred[10]{0:T(512)(128)(4,1)S(1)} %get-tuple-element.177, pred[]{:T(512)S(6)} %compare.3, bf16[10,20,128,128]{3,2,1,0:T(8,128)(2,1)} %get-tuple-element.196, ...), kind=kOutput, calls=%fused_computation.1.clone.1 | convolution fusion | flops 169738240 | bytes 6881803 | tf_op jit(solution)/shard_map/while/body/eval_jaxpr/bij,mbjc->mbic/dot_general | solution.py:59
  181.3 4.1 %bitcast_add_fusion.2 = f32[4,10,128,128]{2,3,0,1:T(8,128)} fusion(f32[4,10,128,128]{2,3,0,1:T(8,128)} %get-tuple-element.186, bf16[10,4,128,128]{3,2,1,0:T(8,128)(2,1)S(1)} %gather_fusion, pred[10]{0:T(512)(128)(4,1)S(1)} %get-tuple-element.177, pred[]{:T(512)S(6)} %compare.3, bf16[10,20,128,128]{3,2,1,0:T(8,128)(2,1)} %get-tuple-element.196, ...), kind=kOutput, calls=%fused_computation.1.clone.1 | convolution fusion | flops 169738240 | bytes 6881803 | tf_op jit(solution)/shard_map/while/body/eval_jaxpr/bij,mbjc->mbic/dot_general | solution.py:59
  185.4 2.9 gather_fusion
  188.3 4.1 %bitcast_add_fusion.2 = f32[4,10,128,128]{2,3,0,1:T(8,128)} fusion(f32[4,10,128,128]{2,3,0,1:T(8,128)} %get-tuple-element.186, bf16[10,4,128,128]{3,2,1,0:T(8,128)(2,1)S(1)} %gather_fusion, pred[10]{0:T(512)(128)(4,1)S(1)} %get-tuple-element.177, pred[]{:T(512)S(6)} %compare.3, bf16[10,20,128,128]{3,2,1,0:T(8,128)(2,1)} %get-tuple-element.196, ...), kind=kOutput, calls=%fused_computation.1.clone.1 | convolution fusion | flops 169738240 | bytes 6881803 | tf_op jit(solution)/shard_map/while/body/eval_jaxpr/bij,mbjc->mbic/dot_general | solution.py:59
  192.4 2.9 gather_fusion
  195.3 4.1 %bitcast_add_fusion.2 = f32[4,10,128,128]{2,3,0,1:T(8,128)} fusion(f32[4,10,128,128]{2,3,0,1:T(8,128)} %get-tuple-element.186, bf16[10,4,128,128]{3,2,1,0:T(8,128)(2,1)S(1)} %gather_fusion, pred[10]{0:T(512)(128)(4,1)S(1)} %get-tuple-element.177, pred[]{:T(512)S(6)} %compare.3, bf16[10,20,128,128]{3,2,1,0:T(8,128)(2,1)} %get-tuple-element.196, ...), kind=kOutput, calls=%fused_computation.1.clone.1 | convolution fusion | flops 169738240 | bytes 6881803 | tf_op jit(solution)/shard_map/while/body/eval_jaxpr/bij,mbjc->mbic/dot_general | solution.py:59
  199.4 2.9 gather_fusion
  202.3 4.1 %bitcast_add_fusion.2 = f32[4,10,128,128]{2,3,0,1:T(8,128)} fusion(f32[4,10,128,128]{2,3,0,1:T(8,128)} %get-tuple-element.186, bf16[10,4,128,128]{3,2,1,0:T(8,128)(2,1)S(1)} %gather_fusion, pred[10]{0:T(512)(128)(4,1)S(1)} %get-tuple-element.177, pred[]{:T(512)S(6)} %compare.3, bf16[10,20,128,128]{3,2,1,0:T(8,128)(2,1)} %get-tuple-element.196, ...), kind=kOutput, calls=%fused_computation.1.clone.1 | convolution fusion | flops 169738240 | bytes 6881803 | tf_op jit(solution)/shard_map/while/body/eval_jaxpr/bij,mbjc->mbic/dot_general | solution.py:59
  206.4 2.9 gather_fusion
  209.3 4.1 %bitcast_add_fusion.2 = f32[4,10,128,128]{2,3,0,1:T(8,128)} fusion(f32[4,10,128,128]{2,3,0,1:T(8,128)} %get-tuple-element.186, bf16[10,4,128,128]{3,2,1,0:T(8,128)(2,1)S(1)} %gather_fusion, pred[10]{0:T(512)(128)(4,1)S(1)} %get-tuple-element.177, pred[]{:T(512)S(6)} %compare.3, bf16[10,20,128,128]{3,2,1,0:T(8,128)(2,1)} %get-tuple-element.196, ...), kind=kOutput, calls=%fused_computation.1.clone.1 | convolution fusion | flops 169738240 | bytes 6881803 | tf_op jit(solution)/shard_map/while/body/eval_jaxpr/bij,mbjc->mbic/dot_general | solution.py:59
  213.4 2.9 gather_fusion
  216.3 4.1 %bitcast_add_fusion.2 = f32[4,10,128,128]{2,3,0,1:T(8,128)} fusion(f32[4,10,128,128]{2,3,0,1:T(8,128)} %get-tuple-element.186, bf16[10,4,128,128]{3,2,1,0:T(8,128)(2,1)S(1)} %gather_fusion, pred[10]{0:T(512)(128)(4,1)S(1)} %get-tuple-element.177, pred[]{:T(512)S(6)} %compare.3, bf16[10,20,128,128]{3,2,1,0:T(8,128)(2,1)} %get-tuple-element.196, ...), kind=kOutput, calls=%fused_computation.1.clone.1 | convolution fusion | flops 169738240 | bytes 6881803 | tf_op jit(solution)/shard_map/while/body/eval_jaxpr/bij,mbjc->mbic/dot_general | solution.py:59
  220.4 2.9 gather_fusion
  223.4 4.1 %bitcast_add_fusion.2 = f32[4,10,128,128]{2,3,0,1:T(8,128)} fusion(f32[4,10,128,128]{2,3,0,1:T(8,128)} %get-tuple-element.186, bf16[10,4,128,128]{3,2,1,0:T(8,128)(2,1)S(1)} %gather_fusion, pred[10]{0:T(512)(128)(4,1)S(1)} %get-tuple-element.177, pred[]{:T(512)S(6)} %compare.3, bf16[10,20,128,128]{3,2,1,0:T(8,128)(2,1)} %get-tuple-element.196, ...), kind=kOutput, calls=%fused_computation.1.clone.1 | convolution fusion | flops 169738240 | bytes 6881803 | tf_op jit(solution)/shard_map/while/body/eval_jaxpr/bij,mbjc->mbic/dot_general | solution.py:59
  227.4 2.9 gather_fusion
  230.4 4.1 %bitcast_add_fusion.2 = f32[4,10,128,128]{2,3,0,1:T(8,128)} fusion(f32[4,10,128,128]{2,3,0,1:T(8,128)} %get-tuple-element.186, bf16[10,4,128,128]{3,2,1,0:T(8,128)(2,1)S(1)} %gather_fusion, pred[10]{0:T(512)(128)(4,1)S(1)} %get-tuple-element.177, pred[]{:T(512)S(6)} %compare.3, bf16[10,20,128,128]{3,2,1,0:T(8,128)(2,1)} %get-tuple-element.196, ...), kind=kOutput, calls=%fused_computation.1.clone.1 | convolution fusion | flops 169738240 | bytes 6881803 | tf_op jit(solution)/shard_map/while/body/eval_jaxpr/bij,mbjc->mbic/dot_general | solution.py:59
  234.4 2.9 gather_fusion
  237.4 4.1 %bitcast_add_fusion.2 = f32[4,10,128,128]{2,3,0,1:T(8,128)} fusion(f32[4,10,128,128]{2,3,0,1:T(8,128)} %get-tuple-element.186, bf16[10,4,128,128]{3,2,1,0:T(8,128)(2,1)S(1)} %gather_fusion, pred[10]{0:T(512)(128)(4,1)S(1)} %get-tuple-element.177, pred[]{:T(512)S(6)} %compare.3, bf16[10,20,128,128]{3,2,1,0:T(8,128)(2,1)} %get-tuple-element.196, ...), kind=kOutput, calls=%fused_computation.1.clone.1 | convolution fusion | flops 169738240 | bytes 6881803 | tf_op jit(solution)/shard_map/while/body/eval_jaxpr/bij,mbjc->mbic/dot_general | solution.py:59
  244.4 4.1 %bitcast_add_fusion.2 = f32[4,10,128,128]{2,3,0,1:T(8,128)} fusion(f32[4,10,128,128]{2,3,0,1:T(8,128)} %get-tuple-element.186, bf16[10,4,128,128]{3,2,1,0:T(8,128)(2,1)S(1)} %gather_fusion, pred[10]{0:T(512)(128)(4,1)S(1)} %get-tuple-element.177, pred[]{:T(512)S(6)} %compare.3, bf16[10,20,128,128]{3,2,1,0:T(8,128)(2,1)} %get-tuple-element.196, ...), kind=kOutput, calls=%fused_computation.1.clone.1 | convolution fusion | flops 169738240 | bytes 6881803 | tf_op jit(solution)/shard_map/while/body/eval_jaxpr/bij,mbjc->mbic/dot_general | solution.py:59
  251.4 4.1 %bitcast_add_fusion.2 = f32[4,10,128,128]{2,3,0,1:T(8,128)} fusion(f32[4,10,128,128]{2,3,0,1:T(8,128)} %get-tuple-element.186, bf16[10,4,128,128]{3,2,1,0:T(8,128)(2,1)S(1)} %gather_fusion, pred[10]{0:T(512)(128)(4,1)S(1)} %get-tuple-element.177, pred[]{:T(512)S(6)} %compare.3, bf16[10,20,128,128]{3,2,1,0:T(8,128)(2,1)} %get-tuple-element.196, ...), kind=kOutput, calls=%fused_computation.1.clone.1 | convolution fusion | flops 169738240 | bytes 6881803 | tf_op jit(solution)/shard_map/while/body/eval_jaxpr/bij,mbjc->mbic/dot_general | solution.py:59
  258.4 4.1 %bitcast_add_fusion.2 = f32[4,10,128,128]{2,3,0,1:T(8,128)} fusion(f32[4,10,128,128]{2,3,0,1:T(8,128)} %get-tuple-element.186, bf16[10,4,128,128]{3,2,1,0:T(8,128)(2,1)S(1)} %gather_fusion, pred[10]{0:T(512)(128)(4,1)S(1)} %get-tuple-element.177, pred[]{:T(512)S(6)} %compare.3, bf16[10,20,128,128]{3,2,1,0:T(8,128)(2,1)} %get-tuple-element.196, ...), kind=kOutput, calls=%fused_computation.1.clone.1 | convolution fusion | flops 169738240 | bytes 6881803 | tf_op jit(solution)/shard_map/while/body/eval_jaxpr/bij,mbjc->mbic/dot_general | solution.py:59
  265.4 4.1 %bitcast_add_fusion.2 = f32[4,10,128,128]{2,3,0,1:T(8,128)} fusion(f32[4,10,128,128]{2,3,0,1:T(8,128)} %get-tuple-element.186, bf16[10,4,128,128]{3,2,1,0:T(8,128)(2,1)S(1)} %gather_fusion, pred[10]{0:T(512)(128)(4,1)S(1)} %get-tuple-element.177, pred[]{:T(512)S(6)} %compare.3, bf16[10,20,128,128]{3,2,1,0:T(8,128)(2,1)} %get-tuple-element.196, ...), kind=kOutput, calls=%fused_computation.1.clone.1 | convolution fusion | flops 169738240 | bytes 6881803 | tf_op jit(solution)/shard_map/while/body/eval_jaxpr/bij,mbjc->mbic/dot_general | solution.py:59
  272.4 4.1 %bitcast_add_fusion.2 = f32[4,10,128,128]{2,3,0,1:T(8,128)} fusion(f32[4,10,128,128]{2,3,0,1:T(8,128)} %get-tuple-element.186, bf16[10,4,128,128]{3,2,1,0:T(8,128)(2,1)S(1)} %gather_fusion, pred[10]{0:T(512)(128)(4,1)S(1)} %get-tuple-element.177, pred[]{:T(512)S(6)} %compare.3, bf16[10,20,128,128]{3,2,1,0:T(8,128)(2,1)} %get-tuple-element.196, ...), kind=kOutput, calls=%fused_computation.1.clone.1 | convolution fusion | flops 169738240 | bytes 6881803 | tf_op jit(solution)/shard_map/while/body/eval_jaxpr/bij,mbjc->mbic/dot_general | solution.py:59
  280.3 71.7 %all-reduce.2.cloned.1.call-done = f32[4,64,128]{2,1,0:T(8,128)} async-done(((f32[4,64,128]{2,1,0:T(8,128)}), f32[4,64,128]{2,1,0:T(8,128)}) %all-reduce.2.cloned.1.call-update) | async-done | bytes 131088 | tf_op jit(solution)/shard_map/psum | solution.py:67
  (71 shorter events, 28.5 us)
Async XLA Ops:
  7.2 272.0 %copy-start = (bf16[1280,64]{0,1:T(8,128)(2,1)S(1)}, bf16[1280,64]{0,1:T(8,128)(2,1)}, u32[]{:S(2)}) copy-start(bf16[1280,64]{0,1:T(8,128)(2,1)} %param.11) | copy-start | bytes 491524
  7.2 66.4 %reduce-scatter.2.cloned.1.call-start = ((), (), s32[]{:S(2)}) async-start(), calls=%async_computation.1 | async-start | bytes 3932160 | tf_op jit(solution)/shard_map/reduce_scatter | solution.py:46
  60.6 18.2 %copy-start.2 = (s32[10,20]{1,0:T(8,128)S(1)}, s32[10,20]{1,0:T(8,128)}, u32[]{:S(2)}) copy-start(s32[10,20]{1,0:T(8,128)} %param.10) | copy-start | bytes 2404
  60.6 291.4 %all-reduce.2.cloned.1.call-start = ((), (), s32[]{:S(2)}) async-start(), calls=%async_computation.2 | async-start | bytes 262144 | tf_op jit(solution)/shard_map/psum | solution.py:67
  73.6 60.5 %collective-permute-start = (bf16[4,1280,128]{2,1,0:T(8,128)(2,1)}, bf16[4,1280,128]{2,1,0:T(8,128)(2,1)S(1)}, u32[]{:S(2)}, u32[]{:S(2)}) collective-permute-start(bf16[4,1280,128]{2,1,0:T(8,128)(2,1)} %reduce-scatter.2.cloned.1.call-done), channel_id=1, source_target_pairs={{0,1},{1,2},{2,3},{3,4},{4,5},{5,6},{6,7},{8,9},{9,10},{10,11},{11... | collective-permute-start | bytes 3932168 | tf_op jit(solution)/shard_map/ppermute | solution.py:16
  77.4 56.7 %collective-permute-start.1 = (bf16[4,1280,128]{2,1,0:T(8,128)(2,1)}, bf16[4,1280,128]{2,1,0:T(8,128)(2,1)S(1)}, u32[]{:S(2)}, u32[]{:S(2)}) collective-permute-start(bf16[4,1280,128]{2,1,0:T(8,128)(2,1)} %reduce-scatter.2.cloned.1.call-done), channel_id=1, source_target_pairs={{1,0},{2,1},{3,2},{4,3},{5,4},{6,5},{7,6},{9,8},{10,9},{11,10},{12... | collective-permute-start | bytes 3932168 | tf_op jit(solution)/shard_map/ppermute | solution.py:19
  279.2 74.4 %copy-start.1 = (bf16[4,10,128,128]{3,2,1,0:T(8,128)(2,1)}, bf16[4,10,128,128]{3,2,1,0:T(8,128)(2,1)S(1)}, u32[]{:S(2)}) copy-start(bf16[4,10,128,128]{3,2,1,0:T(8,128)(2,1)S(1)} %copy.14) | copy-start | bytes 3932164
Sparse Core Ops, SparseCore 0:
  60.7 12.8 reduce-scatter.1
  280.4 71.5 all-reduce.1
where the time goes:
time: 363 us; the launch traced here: 360 us
  waiting for transfers between devices  140 us (39%)
  local copies, waits for them, and re-layouts  94.6 us (26%)
  matrix products  84.7 us (23%)
  other arithmetic  21.4 us (6%)
  between operations  14.1 us (4%)
  starting transfers between devices  5.14 us (1%)
    dot_general x20, matrix products, add_slot(): jnp.einsum('bij,mbjc->mbic', tiles, chosen, preferred_element_type=jnp.fl...  80.2 us
    psum x1, waiting for transfers between devices, local(): reduced = lax.psum(term, 'rows')  71.7 us
    gather x20, local copies, waits for them, and re-layouts, add_slot(): chosen = jnp.take(panel_blocks, columns_now, axis=1)  58.2 us
    ppermute x1, waiting for transfers between devices, with_halo(): lax.ppermute(lax.slice_in_dim(block, block.shape[dim] - width, None, axis...  55.3 us
    reduce_scatter x1, waiting for transfers between devices, local(): lax.psum_scatter(partial_value.astype(jnp.bfloat16), 'quad', scatter_dime...  13 us
    reshape x1, local copies, waits for them, and re-layouts, local(): jnp.concatenate([solutions[:, :, :width], solutions[:, :, width:]], axis=0)  11 us
    concatenate x1, other arithmetic, local(): jnp.concatenate([solutions[:, :, :width], solutions[:, :, width:]], axis=0)  10.4 us
    slice x1, local copies, waits for them, and re-layouts, local(): solutions[:, :, :width]  9.61 us
  transfers between devices with their start and end apart: 4, of which 3 were waited for; matrix products, arithmetic and copies ran while one was open for 0% of the time, Pallas kernels for 0%

commit v1 on v0

v1 whole, which is shorter than its diff:
```python
import functools
import math

import jax
import jax.numpy as jnp
from jax import lax
from jax.experimental import pallas as pl
from jax.experimental.pallas import tpu as pltpu
from jax.sharding import PartitionSpec as P

MOMENTS = 8
TILE = 16
MESH = pl.DeviceIdType.MESH


def kernel(
    n, quads, span, owned, points, chunk_blocks, reduce_here,
    weight_ref, cols_ref, sources_ref, sol_hbm, mass_hbm,
    out_hbm, red_out,
    sol, mass, sources_t, own, theirs, received, out_buf, term, rs_buf, red, *rest,
):
    panels = rest[:owned]
    (sol_sem, mass_sem, out_sem, q_send, q_recv, h_send, h_recv,
     rs_send, rs_recv, ag_send, ag_recv) = rest[owned:]
    me = lax.axis_index("rows")
    quad = lax.axis_index("quad")
    rows_here, lanes = sol.shape[1:]
    half = lanes // 2
    block = rows_here // span
    chunks = span // chunk_blocks
    chunk_rows = chunk_blocks * block
    right = jnp.minimum(me + 1, n - 1)
    left = jnp.maximum(me - 1, 0)

    def sol_copy(c):
        rows = pl.ds(c * chunk_rows, chunk_rows)
        return pltpu.make_async_copy(sol_hbm.at[:, rows], sol.at[:, rows], sol_sem.at[c])

    mass_copy = pltpu.make_async_copy(mass_hbm, mass, mass_sem)
    for c in range(chunks):
        sol_copy(c).start()
    mass_copy.start()

    barrier = pltpu.get_barrier_semaphore()
    pl.semaphore_signal(barrier, inc=1, device_id={"quad": 1 - quad}, device_id_type=MESH)
    if reduce_here:
        for o in range(1, n):
            pl.semaphore_signal(
                barrier, inc=1, device_id={"rows": lax.rem(me + o, n)}, device_id_type=MESH
            )
        pl.semaphore_wait(barrier, n)
    else:
        for o in (1, n - 1):
            pl.semaphore_signal(
                barrier, inc=1, device_id={"rows": lax.rem(me + o, n)}, device_id_type=MESH
            )
        pl.semaphore_wait(barrier, 3)

    def quad_copy(c):
        rows = pl.ds(c * chunk_rows, chunk_rows)
        return pltpu.make_async_remote_copy(
            src_ref=theirs.at[:, rows], dst_ref=received.at[:, rows],
            send_sem=q_send.at[c], recv_sem=q_recv.at[c],
            device_id={"quad": 1 - quad}, device_id_type=MESH,
        )

    pieces = [[(c * chunk_blocks, chunk_blocks) for c in range(chunks)]]
    pieces += [[(0, span)] for _ in range(owned - 1)]
    index_of = {}
    for k in range(owned):
        for p in range(len(pieces[k])):
            index_of[k, p] = len(index_of)

    def halo(k, p, to_right):
        first, count = pieces[k][p]
        source = panels[k].at[pl.ds(span + first, count)]
        target = panels[k].at[pl.ds(first if to_right else 2 * span + first, count)]
        side = 0 if to_right else 1
        at = index_of[k, p]
        return pltpu.make_async_remote_copy(
            src_ref=source, dst_ref=target,
            send_sem=h_send.at[at, side], recv_sem=h_recv.at[at, side],
            device_id={"rows": right if to_right else left}, device_id_type=MESH,
        )

    def halo_start(k, p):
        @pl.when(me < n - 1)
        def _():
            halo(k, p, True).start()

        @pl.when(me > 0)
        def _():
            halo(k, p, False).start()

    def halo_sent(k):
        @pl.when(me < n - 1)
        def _():
            for p in range(len(pieces[k])):
                halo(k, p, True).wait_send()

        @pl.when(me > 0)
        def _():
            for p in range(len(pieces[k])):
                halo(k, p, False).wait_send()

    def halo_arrived(k):
        @pl.when(me > 0)
        def _():
            for p in range(len(pieces[k])):
                halo(k, p, True).wait_recv()

        @pl.when(me < n - 1)
        def _():
            for p in range(len(pieces[k])):
                halo(k, p, False).wait_recv()

    def weigh(c):
        def body(g, carry):
            first = pl.multiple_of(c * chunk_rows + g * 2 * TILE, 2 * TILE)
            second = pl.multiple_of(first + TILE, TILE)
            stacked = jnp.concatenate(
                [
                    sol[:, pl.ds(first, TILE), :].reshape(points * TILE, lanes),
                    sol[:, pl.ds(second, TILE), :].reshape(points * TILE, lanes),
                ],
                axis=1,
            )
            z = jnp.dot(weight_ref[...], stacked, preferred_element_type=jnp.float32)
            height = 2 * owned * TILE
            negative = lax.broadcasted_iota(jnp.int32, (height, lanes), 1) < half
            for h, start in ((0, first), (1, second)):
                straight = z[:height, h * lanes:(h + 1) * lanes]
                crossed = pltpu.roll(z[height:, h * lanes:(h + 1) * lanes], half, 1)
                value = straight + jnp.where(negative, -crossed, crossed)
                value = value.astype(jnp.bfloat16).reshape(2 * owned, TILE, lanes)
                own[:, pl.ds(start, TILE), :] = value[:owned]
                theirs[:, pl.ds(start, TILE), :] = value[owned:]
            return carry

        lax.fori_loop(0, chunk_rows // (2 * TILE), body, 0)

    def add_up(k, first, count):
        def body(b, carry):
            rows = pl.ds(pl.multiple_of(b * block, block), block)
            total = own[k, rows, :].astype(jnp.float32) + received[k, rows, :].astype(jnp.float32)
            panels[k][span + b] = total.astype(jnp.bfloat16)
            return carry

        lax.fori_loop(first, first + count, body, 0)

    def first_moment(c):
        quad_copy(c).wait_recv()
        add_up(0, c * chunk_blocks, chunk_blocks)
        halo_start(0, c)

    for c in range(chunks):
        sol_copy(c).wait()
        weigh(c)
        quad_copy(c).start()
        if c > 0:
            first_moment(c - 1)
    first_moment(chunks - 1)
    for k in range(1, owned):
        add_up(k, 0, span)
        if k == 1:
            halo_start(1, 0)
    sources_t[...] = sources_ref[...].astype(jnp.float32).T.astype(jnp.bfloat16)
    mass_copy.wait()
    slots = mass.shape[1]

    def apply_mass(k):
        panel = panels[k]

        def body(i, carry):
            left_side = jnp.concatenate([mass[i, j] for j in range(slots)], axis=1)
            right_side = jnp.concatenate([panel[cols_ref[i, j]] for j in range(slots)], axis=0)
            value = jnp.dot(left_side, right_side, preferred_element_type=jnp.float32)
            out_buf[k, pl.ds(pl.multiple_of(i * block, block), block), :] = value.astype(jnp.bfloat16)
            return carry

        lax.fori_loop(0, span, body, 0)

    def out_copy(k):
        return pltpu.make_async_copy(out_buf.at[k], out_hbm.at[k], out_sem.at[k])

    def rs_copy(k, o):
        return pltpu.make_async_remote_copy(
            src_ref=term.at[k, lax.rem(me + o, n)], dst_ref=rs_buf.at[k, o],
            send_sem=rs_send.at[k, o], recv_sem=rs_recv.at[k, o],
            device_id={"rows": lax.rem(me + o, n)}, device_id_type=MESH,
        )

    def ag_copy(k, o, origin):
        return pltpu.make_async_remote_copy(
            src_ref=red.at[k, origin], dst_ref=red.at[k, origin],
            send_sem=ag_send.at[k, o], recv_sem=ag_recv.at[k, o],
            device_id={"rows": lax.rem(me + o, n)}, device_id_type=MESH,
        )

    def project(k):
        value = jnp.dot(sources_t[...], out_buf[k], preferred_element_type=jnp.float32)
        if reduce_here:
            term[k] = value.reshape(term.shape[1:])
            for o in range(1, n):
                rs_copy(k, o).start()
        else:
            red_out[k] = value

    def reduce(k):
        total = term[k, me]
        for o in range(1, n):
            rs_copy(k, o).wait_recv()
            total = total + rs_buf[k, o]
        red[k, me] = total
        for o in range(1, n):
            ag_copy(k, o, me).start()

    for k in range(owned):
        if k + 1 < owned:
            if k > 0:
                halo_sent(k - 1)
                halo_start(k + 1, 0)
        halo_arrived(k)
        apply_mass(k)
        out_copy(k).start()
        project(k)
        if reduce_here and k > 0:
            reduce(k - 1)
    if reduce_here:
        reduce(owned - 1)
    for k in range(max(owned - 2, 0), owned):
        halo_sent(k)
    for c in range(chunks):
        quad_copy(c).wait_send()
    for k in range(owned):
        out_copy(k).wait()
        if reduce_here:
            for o in range(1, n):
                rs_copy(k, o).wait_send()
                ag_copy(k, o, me).wait_send()
                ag_copy(k, o, lax.rem(me + n - o, n)).wait_recv()
            red_out[k] = red[k].reshape(red_out.shape[1:])


def local(n, quads, solutions, point_of_slot, mass_blocks, block_cols, sources):
    points, rows_here, lanes = solutions.shape
    width = lanes // 2
    span, slots, block_size = mass_blocks.shape[:3]
    owned = MOMENTS // quads
    total_points = points * quads
    chunk_blocks = 2
    chunks = span // chunk_blocks
    reduce_here = n <= 8 and width % n == 0
    parts = n if reduce_here else 1
    theta = 2.0 * math.pi * (point_of_slot.astype(jnp.float32) + 0.5) / total_points
    order = (jnp.arange(MOMENTS) + owned * lax.axis_index("quad")) % MOMENTS
    angles = (order + 1).astype(jnp.float32)[:, None] * theta[None, :]
    cosine = (jnp.cos(angles) / total_points).astype(jnp.bfloat16)
    sine = (jnp.sin(angles) / total_points).astype(jnp.bfloat16)
    both = jnp.concatenate([cosine, sine], axis=0)
    weight = both[:, None, :, None] * jnp.eye(TILE, dtype=jnp.bfloat16)[None, :, None, :]
    weight = weight.reshape(2 * MOMENTS * TILE, points * TILE)
    cols = block_cols - (lax.axis_index("rows") - 1) * span

    bf16, f32 = jnp.bfloat16, jnp.float32
    dma = pltpu.SemaphoreType.DMA
    pieces = chunks + owned - 1
    vmem = pl.BlockSpec(memory_space=pltpu.VMEM)
    hbm = pl.BlockSpec(memory_space=pl.ANY)
    mass_applied, reduced = pl.pallas_call(
        functools.partial(kernel, n, quads, span, owned, points, chunk_blocks, reduce_here),
        out_shape=(
            jax.ShapeDtypeStruct((owned, rows_here, lanes), bf16),
            jax.ShapeDtypeStruct((owned, width, lanes), f32),
        ),
        in_specs=[vmem, pl.BlockSpec(memory_space=pltpu.SMEM), vmem, hbm, hbm],
        out_specs=(hbm, vmem),
        scratch_shapes=[
            pltpu.VMEM(solutions.shape, bf16),
            pltpu.VMEM(mass_blocks.shape, bf16),
            pltpu.VMEM((width, rows_here), bf16),
            pltpu.VMEM((owned, rows_here, lanes), bf16),
            pltpu.VMEM((owned, rows_here, lanes), bf16),
            pltpu.VMEM((owned, rows_here, lanes), bf16),
            pltpu.VMEM((owned, rows_here, lanes), bf16),
            pltpu.VMEM((owned, parts, width // parts, lanes), f32),
            pltpu.VMEM((owned, parts, width // parts, lanes), f32),
            pltpu.VMEM((owned, parts, width // parts, lanes), f32),
        ]
        + [pltpu.VMEM((3 * span, block_size, lanes), bf16) for _ in range(owned)]
        + [
            dma((chunks,)), dma, dma((owned,)), dma((chunks,)), dma((chunks,)),
            dma((pieces, 2)), dma((pieces, 2)),
            dma((owned, parts)), dma((owned, parts)), dma((owned, parts)), dma((owned, parts)),
        ],
        compiler_params=pltpu.CompilerParams(
            collective_id=0, has_side_effects=True, vmem_limit_bytes=48 * 1024 * 1024
        ),
    )(weight, cols, sources, solutions, mass_blocks)
    if not reduce_here:
        reduced = lax.psum(reduced, "rows")
    return mass_applied, reduced


def solution(mesh):
    in_specs = (
        P("quad", ("group", "rows"), None),
        P(("group", "quad")),
        P(("group", "rows"), None, None, None),
        P(("group", "rows"), None),
        P(("group", "rows"), None),
    )
    out_specs = (P("quad", ("group", "rows"), None), P(("group", "quad"), None, None))
    step = functools.partial(local, mesh.shape["rows"], mesh.shape["quad"])
    return jax.shard_map(step, mesh=mesh, in_specs=in_specs, out_specs=out_specs, check_vma=False)
```

time: 363 us -> 89.7 us (0.25)
  waiting for transfers between devices: 140 us -> 0 us
  local copies, waits for them, and re-layouts: 94.6 us -> 3.83 us
  matrix products: 84.7 us -> 0 us
  Pallas kernels: 0 us -> 83.3 us
  other arithmetic: 21.4 us -> 1.65 us
  between operations: 14.1 us -> 0.67 us
  starting transfers between devices: 5.14 us -> 0 us
    dot_general x22 -> x0, matrix products: 84.7 us -> none  [the longest x20 80.2 us: add_slot(): jnp.einsum('bij,mbjc->mbic', tiles, chosen, preferred_element_type=jnp.fl...]
    pallas_call x0 -> x1, Pallas kernels: none -> 83.3 us  [local(): pl.pallas_call(functools.partial(kernel, n, quads, span, owned, points, c...]
    psum x1 -> x0, waiting for transfers between devices: 71.7 us -> none  [local(): reduced = lax.psum(term, 'rows')]
    gather x20 -> x0, local copies, waits for them, and re-layouts: 58.2 us -> none  [add_slot(): chosen = jnp.take(panel_blocks, columns_now, axis=1)]
    ppermute x2 -> x0, waiting for transfers between devices: 55.3 us -> none  [the longest x1 55.3 us: with_halo(): lax.ppermute(lax.slice_in_dim(block, block.shape[dim] - width, None, axis...]
    concatenate x3 -> x1, other arithmetic: 18.2 us -> 0.01 us  [local(): both = jnp.concatenate([cosine, sine], axis=0)]
    reduce_scatter x1 -> x0, waiting for transfers between devices: 13 us -> none  [local(): lax.psum_scatter(partial_value.astype(jnp.bfloat16), 'quad', scatter_dime...]
    reshape x1 -> x0, local copies, waits for them, and re-layouts: 11 us -> none  [local(): jnp.concatenate([solutions[:, :, :width], solutions[:, :, width:]], axis=0)]
  transfers between devices with their start and end apart: 4 -> 0, of which waited for: 3 -> 0; matrix products, arithmetic and copies ran while one was open for 0% -> 0% of each run, Pallas kernels for 0% -> 0%
where the time goes in v1:
time: 89.7 us; the launch traced here: 89.4 us
  Pallas kernels  83.3 us (93%)
  local copies, waits for them, and re-layouts  3.83 us (4%)
  other arithmetic  1.65 us (2%)
    pallas_call x1, Pallas kernels, local(): pl.pallas_call(functools.partial(kernel, n, quads, span, owned, points, c...  83.3 us
    unnamed x3, local copies, waits for them, and re-layouts  2.85 us

profile of v1, /device:TPU:0, one launch (start us, length us, event | category | flops | bytes accessed | tf_op | source)
XLA Modules:
  0.0 89.4 jit_solution(10239113106944359487)
XLA Ops:
  0.7 0.7 add_multiply_fusion
  1.3 0.1 fusion.2
  1.5 0.7 broadcast_subtract_fusion.cols_ref
  2.2 1.1 %copy.7.sources_ref = bf16[1280,64]{1,0:T(8,128)(2,1)S(1)} copy(bf16[1280,64]{0,1:T(8,128)(2,1)} %param.9) | data formatting | bytes 327680 | tf_op args[4]
  3.3 0.1 broadcast_multiply_fusion
  3.4 1.0 %mul.40.weight_ref = bf16[256,256]{1,0:T(8,128)(2,1)S(1)} reshape(bf16[16,16,16,16]{3,2,1,0:T(8,128)(2,1)S(1)} %broadcast_multiply_fusion) | data formatting | bytes 262144 | tf_op jit(solution)/shard_map/mul | solution.py:261
  4.4 83.3 %shard_map.68 = (bf16[4,1280,128]{2,1,0:T(8,128)(2,1)S(1)}, f32[4,64,128]{2,1,0:T(8,128)S(1)}) custom-call(bf16[256,256]{1,0:T(8,128)(2,1)S(1)} %mul.40.weight_ref, s32[10,20]{1,0:T(8,128)S(1)} %broadcast_subtract_fusion.cols_ref, bf16[1280,64]{1,0:T(8,128)(2,1)S(1)} %copy.7.sources_ref, bf16[16,1280,128]{2,1,0:T(8,128)(2,1)} %sol_hbm.1, ...), custom_call_target="tpu_custom_call" | custom-call | tf_op jit(solution)/shard_map/pallas_call | solution.py:270
  87.7 1.1 %copy.10 = bf16[4,1280,128]{2,1,0:T(8,128)(2,1)} copy(bf16[4,1280,128]{2,1,0:T(8,128)(2,1)S(1)} %get-tuple-element.6) | data formatting | bytes 2621440
  88.8 0.7 copy.11
  (3 shorter events, 0.0 us)

commit v2 on v1

--- a/solution.py
+++ b/solution.py
@@ -10,17 +10,18 @@
 
 MOMENTS = 8
 TILE = 16
+WINDOW = 5
 MESH = pl.DeviceIdType.MESH
 
 
 def kernel(
     n, quads, span, owned, points, chunk_blocks, reduce_here,
-    weight_ref, cols_ref, sources_ref, sol_hbm, mass_hbm,
+    trig_ref, cols_ref, sources_ref, sol_hbm, mass_hbm,
     out_hbm, red_out,
-    sol, mass, sources_t, own, theirs, received, out_buf, term, rs_buf, red, *rest,
+    sol, mass, weight, own, theirs, received, out_buf, term, rs_buf, red, *rest,
 ):
     panels = rest[:owned]
-    (sol_sem, mass_sem, out_sem, q_send, q_recv, h_send, h_recv,
+    (sol_sem, mass_sem, out_sem, q_send, q_recv, x_send, x_recv, f_send, f_recv,
      rs_send, rs_recv, ag_send, ag_recv) = rest[owned:]
     me = lax.axis_index("rows")
     quad = lax.axis_index("quad")
@@ -29,8 +30,13 @@
     block = rows_here // span
     chunks = span // chunk_blocks
     chunk_rows = chunk_blocks * block
-    right = jnp.minimum(me + 1, n - 1)
-    left = jnp.maximum(me - 1, 0)
+    odd = lax.rem(me, 2)
+    partner = me + 1 - 2 * odd
+    onward = lax.rem(me + 2 - 4 * odd + n, n)
+    sends_on = jnp.where(odd == 1, me - 2 >= 0, me + 2 < n)
+    gets_on = jnp.where(odd == 1, me + 2 < n, me - 2 >= 0)
+    there = 2 * span * odd
+    here = 2 * span - there
 
     def sol_copy(c):
         rows = pl.ds(c * chunk_rows, chunk_rows)
@@ -44,17 +50,28 @@
     barrier = pltpu.get_barrier_semaphore()
     pl.semaphore_signal(barrier, inc=1, device_id={"quad": 1 - quad}, device_id_type=MESH)
     if reduce_here:
-        for o in range(1, n):
-            pl.semaphore_signal(
-                barrier, inc=1, device_id={"rows": lax.rem(me + o, n)}, device_id_type=MESH
-            )
-        pl.semaphore_wait(barrier, n)
+        greeted = [lax.rem(me + o, n) for o in range(1, n)]
     else:
-        for o in (1, n - 1):
-            pl.semaphore_signal(
-                barrier, inc=1, device_id={"rows": lax.rem(me + o, n)}, device_id_type=MESH
-            )
-        pl.semaphore_wait(barrier, 3)
+        greeted = [partner, lax.rem(me + 2, n), lax.rem(me + n - 2, n)]
+    for device in greeted:
+        pl.semaphore_signal(barrier, inc=1, device_id={"rows": device}, device_id_type=MESH)
+
+    part = lax.broadcasted_iota(jnp.int32, (2 * 2 * owned * TILE, 2 * 2 * owned), 0)
+    spread = jnp.where(
+        part // TILE == lax.broadcasted_iota(jnp.int32, part.shape, 1), 1.0, 0.0
+    ).astype(jnp.bfloat16)
+    across = lax.broadcasted_iota(jnp.int32, (points * TILE, points), 0)
+    spread_points = jnp.where(
+        across // TILE == lax.broadcasted_iota(jnp.int32, across.shape, 1), 1.0, 0.0
+    ).astype(jnp.bfloat16)
+    tall = jnp.dot(spread, trig_ref[...], preferred_element_type=jnp.float32).astype(jnp.bfloat16)
+    wide = lax.dot_general(
+        tall, spread_points, (((1,), (1,)), ((), ())), preferred_element_type=jnp.float32
+    )
+    same = lax.rem(lax.broadcasted_iota(jnp.int32, wide.shape, 0), TILE) == lax.rem(
+        lax.broadcasted_iota(jnp.int32, wide.shape, 1), TILE
+    )
+    weight[...] = jnp.where(same, wide, 0.0).astype(jnp.bfloat16)
 
     def quad_copy(c):
         rows = pl.ds(c * chunk_rows, chunk_rows)
@@ -64,55 +81,40 @@
             device_id={"quad": 1 - quad}, device_id_type=MESH,
         )
 
-    pieces = [[(c * chunk_blocks, chunk_blocks) for c in range(chunks)]]
-    pieces += [[(0, span)] for _ in range(owned - 1)]
-    index_of = {}
-    for k in range(owned):
-        for p in range(len(pieces[k])):
-            index_of[k, p] = len(index_of)
-
-    def halo(k, p, to_right):
-        first, count = pieces[k][p]
-        source = panels[k].at[pl.ds(span + first, count)]
-        target = panels[k].at[pl.ds(first if to_right else 2 * span + first, count)]
-        side = 0 if to_right else 1
-        at = index_of[k, p]
-        return pltpu.make_async_remote_copy(
-            src_ref=source, dst_ref=target,
-            send_sem=h_send.at[at, side], recv_sem=h_recv.at[at, side],
-            device_id={"rows": right if to_right else left}, device_id_type=MESH,
-        )
-
-    def halo_start(k, p):
-        @pl.when(me < n - 1)
+    pieces = owned * chunks
+
+    def at(q, base):
+        return panels[q // chunks].at[pl.ds(base + q % chunks * chunk_blocks, chunk_blocks)]
+
+    def cross(q, base):
+        return pltpu.make_async_remote_copy(
+            src_ref=at(q, span), dst_ref=at(q, base),
+            send_sem=x_send.at[q], recv_sem=x_recv.at[q],
+            device_id={"rows": partner}, device_id_type=MESH,
+        )
+
+    def forward(q, base):
+        return pltpu.make_async_remote_copy(
+            src_ref=at(q, here), dst_ref=at(q, base),
+            send_sem=f_send.at[q], recv_sem=f_recv.at[q],
+            device_id={"rows": onward}, device_id_type=MESH,
+        )
+
+    def relay(q):
+        cross(q, there).wait_send()
+        if q + WINDOW < pieces:
+            cross(q + WINDOW, there).start()
+        cross(q, here).wait_recv()
+
+        @pl.when(sends_on)
         def _():
-            halo(k, p, True).start()
-
-        @pl.when(me > 0)
+            forward(q, there).start()
+
+    def arrived(k):
+        @pl.when(gets_on)
         def _():
-            halo(k, p, False).start()
-
-    def halo_sent(k):
-        @pl.when(me < n - 1)
-        def _():
-            for p in range(len(pieces[k])):
-                halo(k, p, True).wait_send()
-
-        @pl.when(me > 0)
-        def _():
-            for p in range(len(pieces[k])):
-                halo(k, p, False).wait_send()
-
-    def halo_arrived(k):
-        @pl.when(me > 0)
-        def _():
-            for p in range(len(pieces[k])):
-                halo(k, p, True).wait_recv()
-
-        @pl.when(me < n - 1)
-        def _():
-            for p in range(len(pieces[k])):
-                halo(k, p, False).wait_recv()
+            for p in range(chunks):
+                forward(k * chunks + p, there).wait_recv()
 
     def weigh(c):
         def body(g, carry):
@@ -125,7 +127,7 @@
                 ],
                 axis=1,
             )
-            z = jnp.dot(weight_ref[...], stacked, preferred_element_type=jnp.float32)
+            z = jnp.dot(weight[...], stacked, preferred_element_type=jnp.float32)
             height = 2 * owned * TILE
             negative = lax.broadcasted_iota(jnp.int32, (height, lanes), 1) < half
             for h, start in ((0, first), (1, second)):
@@ -151,34 +153,34 @@
     def first_moment(c):
         quad_copy(c).wait_recv()
         add_up(0, c * chunk_blocks, chunk_blocks)
-        halo_start(0, c)
+        if c < WINDOW:
+            cross(c, there).start()
 
     for c in range(chunks):
         sol_copy(c).wait()
         weigh(c)
+        if c == 0:
+            pl.semaphore_wait(barrier, 1 + len(greeted))
         quad_copy(c).start()
         if c > 0:
             first_moment(c - 1)
     first_moment(chunks - 1)
-    for k in range(1, owned):
-        add_up(k, 0, span)
-        if k == 1:
-            halo_start(1, 0)
-    sources_t[...] = sources_ref[...].astype(jnp.float32).T.astype(jnp.bfloat16)
-    mass_copy.wait()
     slots = mass.shape[1]
-
-    def apply_mass(k):
+    offset = (me - 1) * span
+
+    def apply_mass(k, first, last):
         panel = panels[k]
 
         def body(i, carry):
             left_side = jnp.concatenate([mass[i, j] for j in range(slots)], axis=1)
-            right_side = jnp.concatenate([panel[cols_ref[i, j]] for j in range(slots)], axis=0)
+            right_side = jnp.concatenate(
+                [panel[jnp.clip(cols_ref[i, j] - offset, 0, 3 * span - 1)] for j in range(slots)], axis=0
+            )
             value = jnp.dot(left_side, right_side, preferred_element_type=jnp.float32)
             out_buf[k, pl.ds(pl.multiple_of(i * block, block), block), :] = value.astype(jnp.bfloat16)
             return carry
 
-        lax.fori_loop(0, span, body, 0)
+        lax.fori_loop(first, last, body, 0)
 
     def out_copy(k):
         return pltpu.make_async_copy(out_buf.at[k], out_hbm.at[k], out_sem.at[k])
@@ -198,7 +200,7 @@
         )
 
     def project(k):
-        value = jnp.dot(sources_t[...], out_buf[k], preferred_element_type=jnp.float32)
+        value = jnp.dot(sources_ref[...], out_buf[k], preferred_element_type=jnp.float32)
         if reduce_here:
             term[k] = value.reshape(term.shape[1:])
             for o in range(1, n):
@@ -215,21 +217,39 @@
         for o in range(1, n):
             ag_copy(k, o, me).start()
 
-    for k in range(owned):
-        if k + 1 < owned:
-            if k > 0:
-                halo_sent(k - 1)
-                halo_start(k + 1, 0)
-        halo_arrived(k)
-        apply_mass(k)
+    def finish(k):
         out_copy(k).start()
         project(k)
-        if reduce_here and k > 0:
-            reduce(k - 1)
+
+    cuts = [0, 4, 7, span]
+    for k in range(owned):
+        for p in range(chunks):
+            q = k * chunks + p
+            if k == 0 and p < owned - 1:
+                add_up(p + 1, 0, span)
+            relay(q)
+            if k > 0 and p >= 2:
+                if p == 2:
+                    arrived(k - 1)
+                    if k == 1:
+                        mass_copy.wait()
+                apply_mass(k - 1, cuts[p - 2], cuts[p - 1])
+        if k > 0:
+            finish(k - 1)
+        if reduce_here and k > 1:
+            reduce(k - 2)
+    arrived(owned - 1)
+    apply_mass(owned - 1, 0, span)
+    finish(owned - 1)
     if reduce_here:
+        reduce(owned - 2)
         reduce(owned - 1)
-    for k in range(max(owned - 2, 0), owned):
-        halo_sent(k)
+
+    @pl.when(sends_on)
+    def _():
+        for q in range(pieces):
+            forward(q, there).wait_send()
+
     for c in range(chunks):
         quad_copy(c).wait_send()
     for k in range(owned):
@@ -258,13 +278,9 @@
     cosine = (jnp.cos(angles) / total_points).astype(jnp.bfloat16)
     sine = (jnp.sin(angles) / total_points).astype(jnp.bfloat16)
     both = jnp.concatenate([cosine, sine], axis=0)
-    weight = both[:, None, :, None] * jnp.eye(TILE, dtype=jnp.bfloat16)[None, :, None, :]
-    weight = weight.reshape(2 * MOMENTS * TILE, points * TILE)
-    cols = block_cols - (lax.axis_index("rows") - 1) * span
-
     bf16, f32 = jnp.bfloat16, jnp.float32
     dma = pltpu.SemaphoreType.DMA
-    pieces = chunks + owned - 1
+    pieces = chunks * owned
     vmem = pl.BlockSpec(memory_space=pltpu.VMEM)
     hbm = pl.BlockSpec(memory_space=pl.ANY)
     mass_applied, reduced = pl.pallas_call(
@@ -278,7 +294,7 @@
         scratch_shapes=[
             pltpu.VMEM(solutions.shape, bf16),
             pltpu.VMEM(mass_blocks.shape, bf16),
-            pltpu.VMEM((width, rows_here), bf16),
+            pltpu.VMEM((2 * MOMENTS * TILE, points * TILE), bf16),
             pltpu.VMEM((owned, rows_here, lanes), bf16),
             pltpu.VMEM((owned, rows_here, lanes), bf16),
             pltpu.VMEM((owned, rows_here, lanes), bf16),
@@ -290,13 +306,13 @@
         + [pltpu.VMEM((3 * span, block_size, lanes), bf16) for _ in range(owned)]
         + [
             dma((chunks,)), dma, dma((owned,)), dma((chunks,)), dma((chunks,)),
-            dma((pieces, 2)), dma((pieces, 2)),
+            dma((pieces,)), dma((pieces,)), dma((pieces,)), dma((pieces,)),
             dma((owned, parts)), dma((owned, parts)), dma((owned, parts)), dma((owned, parts)),
         ],
         compiler_params=pltpu.CompilerParams(
             collective_id=0, has_side_effects=True, vmem_limit_bytes=48 * 1024 * 1024
         ),
-    )(weight, cols, sources, solutions, mass_blocks)
+    )(both, block_cols, sources.T, solutions, mass_blocks)
     if not reduce_here:
         reduced = lax.psum(reduced, "rows")
     return mass_applied, reduced

time: 89.7 us -> 67.5 us (0.75)
  Pallas kernels: 83.3 us -> 62.5 us
    pallas_call x1, Pallas kernels: 83.3 us -> 62.5 us  [local(): pl.pallas_call(functools.partial(kernel, n, quads, span, owned, points, c...]
    mul x1 -> x0, local copies, waits for them, and re-layouts: 0.99 us -> none  [local(): both[:, None, :, None] * jnp.eye(TILE, dtype=jnp.bfloat16)[None, :, None, :]]
    unnamed x3 -> x6, local copies, waits for them, and re-layouts: 2.85 us -> 3.32 us
where the time goes in v2:
time: 67.5 us; the launch traced here: 67.3 us
  Pallas kernels  62.5 us (93%)
  local copies, waits for them, and re-layouts  3.32 us (5%)
  other arithmetic  0.8 us (1%)
    pallas_call x1, Pallas kernels, local(): pl.pallas_call(functools.partial(kernel, n, quads, span, owned, points, c...  62.5 us
    unnamed x6, local copies, waits for them, and re-layouts  3.32 us

profile of v2, /device:TPU:0, one launch (start us, length us, event | category | flops | bytes accessed | tf_op | source)
XLA Modules:
  0.0 67.3 jit_solution(1644754672801213786)
XLA Ops:
  0.6 0.7 add_multiply_fusion
  1.3 0.1 fusion.1
  1.4 0.0 copy-start
  1.4 0.9 %copy-done = bf16[1280,64]{0,1:T(8,128)(2,1)S(1)} copy-done((bf16[1280,64]{0,1:T(8,128)(2,1)S(1)}, bf16[1280,64]{0,1:T(8,128)(2,1)}, u32[]{:S(2)}) %copy-start) | copy-done | bytes 163864
  2.4 0.0 copy-start.1
  2.4 0.7 %copy-done.1 = s32[10,20]{1,0:T(8,128)S(1)} copy-done((s32[10,20]{1,0:T(8,128)S(1)}, s32[10,20]{1,0:T(8,128)}, u32[]{:S(2)}) %copy-start.1) | copy-done | bytes 824
  3.1 62.5 %shard_map.68 = (bf16[4,1280,128]{2,1,0:T(8,128)(2,1)S(1)}, f32[4,64,128]{2,1,0:T(8,128)S(1)}) custom-call(bf16[16,16]{1,0:T(8,128)(2,1)S(1)} %pad_maximum_fusion.trig_ref, s32[10,20]{1,0:T(8,128)S(1)} %copy-done.1, bf16[64,1280]{1,0:T(8,128)(2,1)S(1)} %bitcast.1, bf16[16,1280,128]{2,1,0:T(8,128)(2,1)} %sol_hbm.1, bf16[10,20,128,128]{3,2,1,0:T(8,128)(2,1)} %mass_hbm.1), custom_call_target="tpu_custom_call" | custom-call | tf_op jit(solution)/shard_map/pallas_call | solution.py:286
  65.6 1.1 %copy.9 = bf16[4,1280,128]{2,1,0:T(8,128)(2,1)} copy(bf16[4,1280,128]{2,1,0:T(8,128)(2,1)S(1)} %get-tuple-element.6) | data formatting | bytes 2621440
  66.7 0.7 copy.10
  (2 shorter events, 0.0 us)
Async XLA Ops:
  1.4 0.9 %copy-start = (bf16[1280,64]{0,1:T(8,128)(2,1)S(1)}, bf16[1280,64]{0,1:T(8,128)(2,1)}, u32[]{:S(2)}) copy-start(bf16[1280,64]{0,1:T(8,128)(2,1)} %param.9) | copy-start | bytes 491524
  2.4 0.7 %copy-start.1 = (s32[10,20]{1,0:T(8,128)S(1)}, s32[10,20]{1,0:T(8,128)}, u32[]{:S(2)}) copy-start(s32[10,20]{1,0:T(8,128)} %cols_ref.1) | copy-start | bytes 2404

commit v3 on v2

--- a/solution.py
+++ b/solution.py
@@ -10,7 +10,7 @@
 
 MOMENTS = 8
 TILE = 16
-WINDOW = 5
+WINDOW = 3
 MESH = pl.DeviceIdType.MESH
 
 
@@ -82,9 +82,13 @@
         )
 
     pieces = owned * chunks
+    early = 2
+    order = [(k, c) for c in range(chunks) for k in range(early)]
+    order += [(k, c) for k in range(early, owned) for c in range(chunks)]
 
     def at(q, base):
-        return panels[q // chunks].at[pl.ds(base + q % chunks * chunk_blocks, chunk_blocks)]
+        k, c = order[q]
+        return panels[k].at[pl.ds(base + c * chunk_blocks, chunk_blocks)]
 
     def cross(q, base):
         return pltpu.make_async_remote_copy(
@@ -102,7 +106,7 @@
 
     def relay(q):
         cross(q, there).wait_send()
-        if q + WINDOW < pieces:
+        if early * chunks <= q + WINDOW < pieces:
             cross(q + WINDOW, there).start()
         cross(q, here).wait_recv()
 
@@ -114,10 +118,10 @@
         @pl.when(gets_on)
         def _():
             for p in range(chunks):
-                forward(k * chunks + p, there).wait_recv()
+                forward(order.index((k, p)), there).wait_recv()
 
     def weigh(c):
-        def body(g, carry):
+        def pair(g):
             first = pl.multiple_of(c * chunk_rows + g * 2 * TILE, 2 * TILE)
             second = pl.multiple_of(first + TILE, TILE)
             stacked = jnp.concatenate(
@@ -137,9 +141,13 @@
                 value = value.astype(jnp.bfloat16).reshape(2 * owned, TILE, lanes)
                 own[:, pl.ds(start, TILE), :] = value[:owned]
                 theirs[:, pl.ds(start, TILE), :] = value[owned:]
+
+        def body(g, carry):
+            pair(2 * g)
+            pair(2 * g + 1)
             return carry
 
-        lax.fori_loop(0, chunk_rows // (2 * TILE), body, 0)
+        lax.fori_loop(0, chunk_rows // (4 * TILE), body, 0)
 
     def add_up(k, first, count):
         def body(b, carry):
@@ -152,9 +160,9 @@
 
     def first_moment(c):
         quad_copy(c).wait_recv()
-        add_up(0, c * chunk_blocks, chunk_blocks)
-        if c < WINDOW:
-            cross(c, there).start()
+        for k in range(early):
+            add_up(k, c * chunk_blocks, chunk_blocks)
+            cross(order.index((k, c)), there).start()
 
     for c in range(chunks):
         sol_copy(c).wait()
@@ -171,79 +179,82 @@
     def apply_mass(k, first, last):
         panel = panels[k]
 
-        def body(i, carry):
+        def block_row(i):
             left_side = jnp.concatenate([mass[i, j] for j in range(slots)], axis=1)
             right_side = jnp.concatenate(
-                [panel[jnp.clip(cols_ref[i, j] - offset, 0, 3 * span - 1)] for j in range(slots)], axis=0
+                [panel[jnp.clip(cols_ref[i, j] - offset, 0, 3 * span - 1)] for j in range(slots)],
+                axis=0,
             )
             value = jnp.dot(left_side, right_side, preferred_element_type=jnp.float32)
             out_buf[k, pl.ds(pl.multiple_of(i * block, block), block), :] = value.astype(jnp.bfloat16)
+
+        def body(i, carry):
+            block_row(2 * i)
+            block_row(2 * i + 1)
             return carry
 
-        lax.fori_loop(first, last, body, 0)
+        lax.fori_loop(first // 2, last // 2, body, 0)
 
     def out_copy(k):
         return pltpu.make_async_copy(out_buf.at[k], out_hbm.at[k], out_sem.at[k])
 
-    def rs_copy(k, o):
-        return pltpu.make_async_remote_copy(
-            src_ref=term.at[k, lax.rem(me + o, n)], dst_ref=rs_buf.at[k, o],
-            send_sem=rs_send.at[k, o], recv_sem=rs_recv.at[k, o],
+    batches = [pl.ds(0, owned - 1), pl.ds(owned - 1, 1)]
+
+    def rs_copy(b, o):
+        return pltpu.make_async_remote_copy(
+            src_ref=term.at[batches[b], lax.rem(me + o, n)], dst_ref=rs_buf.at[batches[b], o],
+            send_sem=rs_send.at[b, o], recv_sem=rs_recv.at[b, o],
             device_id={"rows": lax.rem(me + o, n)}, device_id_type=MESH,
         )
 
-    def ag_copy(k, o, origin):
-        return pltpu.make_async_remote_copy(
-            src_ref=red.at[k, origin], dst_ref=red.at[k, origin],
-            send_sem=ag_send.at[k, o], recv_sem=ag_recv.at[k, o],
+    def ag_copy(b, o, origin):
+        return pltpu.make_async_remote_copy(
+            src_ref=red.at[batches[b], origin], dst_ref=red.at[batches[b], origin],
+            send_sem=ag_send.at[b, o], recv_sem=ag_recv.at[b, o],
             device_id={"rows": lax.rem(me + o, n)}, device_id_type=MESH,
         )
-
-    def project(k):
-        value = jnp.dot(sources_ref[...], out_buf[k], preferred_element_type=jnp.float32)
-        if reduce_here:
-            term[k] = value.reshape(term.shape[1:])
-            for o in range(1, n):
-                rs_copy(k, o).start()
-        else:
-            red_out[k] = value
-
-    def reduce(k):
-        total = term[k, me]
-        for o in range(1, n):
-            rs_copy(k, o).wait_recv()
-            total = total + rs_buf[k, o]
-        red[k, me] = total
-        for o in range(1, n):
-            ag_copy(k, o, me).start()
 
     def finish(k):
         out_copy(k).start()
-        project(k)
-
-    cuts = [0, 4, 7, span]
-    for k in range(owned):
-        for p in range(chunks):
-            q = k * chunks + p
-            if k == 0 and p < owned - 1:
-                add_up(p + 1, 0, span)
-            relay(q)
-            if k > 0 and p >= 2:
-                if p == 2:
-                    arrived(k - 1)
-                    if k == 1:
-                        mass_copy.wait()
-                apply_mass(k - 1, cuts[p - 2], cuts[p - 1])
-        if k > 0:
-            finish(k - 1)
-        if reduce_here and k > 1:
-            reduce(k - 2)
+        value = jnp.dot(sources_ref[...], out_buf[k], preferred_element_type=jnp.float32)
+        if not reduce_here:
+            red_out[k] = value
+            return
+        term[k] = value.reshape(term.shape[1:])
+        if k >= owned - 2:
+            for o in range(1, n):
+                rs_copy(k - (owned - 2), o).start()
+
+    def reduce(b):
+        total = term[batches[b], me]
+        for o in range(1, n):
+            rs_copy(b, o).wait_recv()
+            total = total + rs_buf[batches[b], o]
+        red[batches[b], me] = total
+        for o in range(1, n):
+            ag_copy(b, o, me).start()
+
+    cuts = [0, 4, 8, span]
+    steps = len(cuts) - 1
+    for q in range(pieces):
+        relay(q)
+        if q % 2 == 1 and early + q // 2 < owned:
+            add_up(early + q // 2, 0, span)
+        if q == early * chunks:
+            mass_copy.wait()
+        k, step = divmod(q - early * chunks, steps)
+        if 0 <= k < owned - 1:
+            if step == 0:
+                arrived(k)
+            apply_mass(k, cuts[step], cuts[step + 1])
+            if step == steps - 1:
+                finish(k)
     arrived(owned - 1)
     apply_mass(owned - 1, 0, span)
     finish(owned - 1)
     if reduce_here:
-        reduce(owned - 2)
-        reduce(owned - 1)
+        reduce(0)
+        reduce(1)
 
     @pl.when(sends_on)
     def _():
@@ -254,11 +265,13 @@
         quad_copy(c).wait_send()
     for k in range(owned):
         out_copy(k).wait()
-        if reduce_here:
+    if reduce_here:
+        for b in range(len(batches)):
             for o in range(1, n):
-                rs_copy(k, o).wait_send()
-                ag_copy(k, o, me).wait_send()
-                ag_copy(k, o, lax.rem(me + n - o, n)).wait_recv()
+                rs_copy(b, o).wait_send()
+                ag_copy(b, o, me).wait_send()
+                ag_copy(b, o, lax.rem(me + n - o, n)).wait_recv()
+        for k in range(owned):
             red_out[k] = red[k].reshape(red_out.shape[1:])
 
 

time: 67.5 us -> 63.8 us (0.945)
  Pallas kernels: 62.5 us -> 58.8 us
    pallas_call x1, Pallas kernels: 62.5 us -> 58.8 us  [local(): pl.pallas_call(functools.partial(kernel, n, quads, span, owned, points, c...]
where the time goes in v3:
time: 63.8 us; the launch traced here: 63.6 us
  Pallas kernels  58.8 us (92%)
  local copies, waits for them, and re-layouts  3.32 us (5%)
  other arithmetic  0.8 us (1%)
  between operations  0.66 us (1%)
    pallas_call x1, Pallas kernels, local(): pl.pallas_call(functools.partial(kernel, n, quads, span, owned, points, c...  58.8 us
    unnamed x6, local copies, waits for them, and re-layouts  3.32 us

profile of v3, /device:TPU:0, one launch (start us, length us, event | category | flops | bytes accessed | tf_op | source)
XLA Modules:
  0.0 63.6 jit_solution(4586362459087565487)
XLA Ops:
  0.6 0.7 %add_multiply_fusion = f32[16]{0:T(128)S(1)} fusion(s32[16]{0:T(128)} %param.6), kind=kLoop, calls=%fused_computation.13 | loop fusion | flops 48 | bytes 128 | tf_op jit(solution)/shard_map/div | solution.py:288
  1.3 0.1 fusion.1
  1.4 0.0 copy-start
  1.4 0.9 %copy-done = bf16[1280,64]{0,1:T(8,128)(2,1)S(1)} copy-done((bf16[1280,64]{0,1:T(8,128)(2,1)S(1)}, bf16[1280,64]{0,1:T(8,128)(2,1)}, u32[]{:S(2)}) %copy-start) | copy-done | bytes 163864
  2.4 0.0 copy-start.1
  2.4 0.7 %copy-done.1 = s32[10,20]{1,0:T(8,128)S(1)} copy-done((s32[10,20]{1,0:T(8,128)S(1)}, s32[10,20]{1,0:T(8,128)}, u32[]{:S(2)}) %copy-start.1) | copy-done | bytes 824
  3.1 58.8 %shard_map.68 = (bf16[4,1280,128]{2,1,0:T(8,128)(2,1)S(1)}, f32[4,64,128]{2,1,0:T(8,128)S(1)}) custom-call(bf16[16,16]{1,0:T(8,128)(2,1)S(1)} %pad_maximum_fusion.trig_ref, s32[10,20]{1,0:T(8,128)S(1)} %copy-done.1, bf16[64,1280]{1,0:T(8,128)(2,1)S(1)} %bitcast.1, bf16[16,1280,128]{2,1,0:T(8,128)(2,1)} %sol_hbm.1, bf16[10,20,128,128]{3,2,1,0:T(8,128)(2,1)} %mass_hbm.1), custom_call_target="tpu_custom_call" | custom-call | tf_op jit(solution)/shard_map/pallas_call | solution.py:299
  61.8 1.1 %copy.9 = bf16[4,1280,128]{2,1,0:T(8,128)(2,1)} copy(bf16[4,1280,128]{2,1,0:T(8,128)(2,1)S(1)} %get-tuple-element.6) | data formatting | bytes 2621440
  62.9 0.7 %copy.10 = f32[4,64,128]{2,1,0:T(8,128)} copy(f32[4,64,128]{2,1,0:T(8,128)S(1)} %get-tuple-element.7) | data formatting | bytes 262144
  (2 shorter events, 0.0 us)
Async XLA Ops:
  1.4 0.9 %copy-start = (bf16[1280,64]{0,1:T(8,128)(2,1)S(1)}, bf16[1280,64]{0,1:T(8,128)(2,1)}, u32[]{:S(2)}) copy-start(bf16[1280,64]{0,1:T(8,128)(2,1)} %param.9) | copy-start | bytes 491524
  2.4 0.7 %copy-start.1 = (s32[10,20]{1,0:T(8,128)S(1)}, s32[10,20]{1,0:T(8,128)}, u32[]{:S(2)}) copy-start(s32[10,20]{1,0:T(8,128)} %cols_ref.1) | copy-start | bytes 2404

commit v4 on v3

--- a/solution.py
+++ b/solution.py
@@ -10,7 +10,7 @@
 
 MOMENTS = 8
 TILE = 16
-WINDOW = 3
+WINDOW = 5
 MESH = pl.DeviceIdType.MESH
 
 
@@ -250,10 +250,12 @@
             if step == steps - 1:
                 finish(k)
     arrived(owned - 1)
-    apply_mass(owned - 1, 0, span)
+    apply_mass(owned - 1, 0, cuts[2])
+    if reduce_here:
+        reduce(0)
+    apply_mass(owned - 1, cuts[2], span)
     finish(owned - 1)
     if reduce_here:
-        reduce(0)
         reduce(1)
 
     @pl.when(sends_on)

time: 63.8 us -> 63.4 us (level)
  no operation moved by 1% of the time
where the time goes in v4:
time: 63.4 us; the launch traced here: 63.2 us
  Pallas kernels  58.5 us (92%)
  local copies, waits for them, and re-layouts  3.32 us (5%)
  other arithmetic  0.8 us (1%)
  between operations  0.66 us (1%)
    pallas_call x1, Pallas kernels, local(): pl.pallas_call(functools.partial(kernel, n, quads, span, owned, points, c...  58.5 us
    unnamed x6, local copies, waits for them, and re-layouts  3.32 us

profile of v4, /device:TPU:0, one launch (start us, length us, event | category | flops | bytes accessed | tf_op | source)
XLA Modules:
  0.0 63.2 jit_solution(3351660959362161674)
XLA Ops:
  0.6 0.7 %add_multiply_fusion = f32[16]{0:T(128)S(1)} fusion(s32[16]{0:T(128)} %param.6), kind=kLoop, calls=%fused_computation.13 | loop fusion | flops 48 | bytes 128 | tf_op jit(solution)/shard_map/div | solution.py:290
  1.3 0.1 fusion.1
  1.4 0.0 copy-start
  1.4 0.9 %copy-done = bf16[1280,64]{0,1:T(8,128)(2,1)S(1)} copy-done((bf16[1280,64]{0,1:T(8,128)(2,1)S(1)}, bf16[1280,64]{0,1:T(8,128)(2,1)}, u32[]{:S(2)}) %copy-start) | copy-done | bytes 163864
  2.4 0.0 copy-start.1
  2.4 0.7 %copy-done.1 = s32[10,20]{1,0:T(8,128)S(1)} copy-done((s32[10,20]{1,0:T(8,128)S(1)}, s32[10,20]{1,0:T(8,128)}, u32[]{:S(2)}) %copy-start.1) | copy-done | bytes 824
  3.1 58.5 %shard_map.68 = (bf16[4,1280,128]{2,1,0:T(8,128)(2,1)S(1)}, f32[4,64,128]{2,1,0:T(8,128)S(1)}) custom-call(bf16[16,16]{1,0:T(8,128)(2,1)S(1)} %pad_maximum_fusion.trig_ref, s32[10,20]{1,0:T(8,128)S(1)} %copy-done.1, bf16[64,1280]{1,0:T(8,128)(2,1)S(1)} %bitcast.1, bf16[16,1280,128]{2,1,0:T(8,128)(2,1)} %sol_hbm.1, bf16[10,20,128,128]{3,2,1,0:T(8,128)(2,1)} %mass_hbm.1), custom_call_target="tpu_custom_call" | custom-call | tf_op jit(solution)/shard_map/pallas_call | solution.py:301
  61.5 1.1 %copy.9 = bf16[4,1280,128]{2,1,0:T(8,128)(2,1)} copy(bf16[4,1280,128]{2,1,0:T(8,128)(2,1)S(1)} %get-tuple-element.6) | data formatting | bytes 2621440
  62.6 0.7 %copy.10 = f32[4,64,128]{2,1,0:T(8,128)} copy(f32[4,64,128]{2,1,0:T(8,128)S(1)} %get-tuple-element.7) | data formatting | bytes 262144
  (2 shorter events, 0.0 us)
Async XLA Ops:
  1.4 0.9 %copy-start = (bf16[1280,64]{0,1:T(8,128)(2,1)S(1)}, bf16[1280,64]{0,1:T(8,128)(2,1)}, u32[]{:S(2)}) copy-start(bf16[1280,64]{0,1:T(8,128)(2,1)} %param.9) | copy-start | bytes 491524
  2.4 0.7 %copy-start.1 = (s32[10,20]{1,0:T(8,128)S(1)}, s32[10,20]{1,0:T(8,128)}, u32[]{:S(2)}) copy-start(s32[10,20]{1,0:T(8,128)} %cols_ref.1) | copy-start | bytes 2404
